TPU v7x, 1024 devices: a whole 8x8x8 slice. The times are simulated.
1024 devices in a mesh: row: 32 (over x, z_hi), grp: 16 (over y, z_lo), col: 2 (over core).
Axes of the slice: x: 8, y: 8, z: 8 (z_hi: 4, z_lo: 2; z = z_hi * 2 + z_lo), core: 2. Of those that a mesh axis runs over, the one named last changes fastest.
Arguments:
- state: float32 [512, 512, 256], P('row', ('grp', 'col')), may hold values from -6 to 6
- rate: float32 [512, 512], P('row', ('grp', 'col')), may hold values from 0.02 to 0.24
- cotangent: bfloat16 [512, 512, 256], P('row', ('grp', 'col')), may hold values from -6 to 6
- dest: int32 [32, 32, 256, 1], P('row', ('grp', 'col')), may hold values from 0 to 15; in each aligned block of 256 rows (0 to 255, 256 to 511, ..., all dimensions but the last counted through in order) at most 32 rows name the same one
- w_in: bfloat16 [16, 256, 1024], P('grp'), may hold values from -0.375 to 0.375
- w_out: bfloat16 [16, 256, 1024], P('grp'), may hold values from -0.1875 to 0.1875
Outputs:
- new_state: float32 [512, 512, 256], P('row', ('grp', 'col'))
- column_adjoint: bfloat16 [512, 512, 256], P('row', ('grp', 'col'))
- weight_grads: float32 [16, 4096, 128], P('grp', ('row', 'col'))
Inputs may be any that keep to these rules, and one draw needn't show every extreme that they name: `dest`: within one block no owner receives more than 32 columns, and some owner receives exactly 32 in some block.
All inputs are finite; a program needn't handle non-finite values.
Results may differ from a plain program's by a relative error of at most 0.0053.
Values may be sent and summed in bfloat16 or wider, within the bound.
A program may use at most 32 MiB of HBM per device.

v0:
```python
import jax
import jax.numpy as jnp
from jax import lax
from jax.sharding import PartitionSpec as P

STEPS = 4


def padded_2(cells, sides, width):
    for axis, dim in sides:
        count = lax.axis_size(axis)
        head = lax.slice_in_dim(cells, 0, width, axis=dim)
        tail = lax.slice_in_dim(cells, cells.shape[dim] - width, cells.shape[dim], axis=dim)
        cells = jnp.concatenate(
            [
                lax.ppermute(tail, axis, [(i, (i + 1) % count) for i in range(count)]),
                cells,
                lax.ppermute(head, axis, [((i + 1) % count, i) for i in range(count)]),
            ],
            axis=dim,
        )
    return cells


def silu_slope(value):
    logistic = jax.nn.sigmoid(value)
    return logistic * (1.0 + value * (1.0 - logistic))


def local(state, rate, cotangent, dest, w_in, w_out):
    rows_blk, cols_blk, feats = state.shape
    count = rows_blk * cols_blk
    owners = lax.axis_size("grp")
    capacity = 2 * count // owners
    routes = dest.reshape(count)
    onehot = (routes[:, None] == jnp.arange(owners, dtype=jnp.int32)[None, :]).astype(jnp.int32)
    ranks = jnp.cumsum(onehot, axis=0) - 1
    places = routes * capacity + jnp.sum(ranks * onehot, axis=1)
    placing = (jnp.arange(owners * capacity, dtype=jnp.int32)[:, None] == places[None, :]).astype(
        jnp.bfloat16
    )
    columns = state.astype(jnp.bfloat16).reshape(count, feats)
    cotans = cotangent.reshape(count, feats)
    packed_cols = jnp.dot(placing, columns, preferred_element_type=jnp.float32).astype(jnp.bfloat16)
    packed_cots = jnp.dot(placing, cotans, preferred_element_type=jnp.float32).astype(jnp.bfloat16)
    recv_cols, recv_cots = (
        lax.all_to_all(
            packed_cols.reshape(owners, capacity, feats),
            "grp",
            split_axis=0,
            concat_axis=0,
            tiled=True,
        ),
        lax.all_to_all(
            packed_cots.reshape(owners, capacity, feats),
            "grp",
            split_axis=0,
            concat_axis=0,
            tiled=True,
        ),
    )
    owner_cols = recv_cols.reshape(owners * capacity, feats)
    owner_cots = recv_cots.reshape(owners * capacity, feats)
    field = state
    for step in range(STEPS):
        padded = padded_2(field.astype(jnp.bfloat16), (("row", 0), (("grp", "col"), 1)), 1).astype(
            field.dtype
        )
        beside = padded[2:, 1:-1] + padded[:-2, 1:-1] + padded[1:-1, 2:] + padded[1:-1, :-2]
        field = field + rate[:, :, None] * (beside - 4.0 * field)
    weight_in = w_in[0]
    weight_out = w_out[0]
    pre = jnp.dot(owner_cols, weight_in, preferred_element_type=jnp.float32)
    act = jax.nn.silu(pre).astype(jnp.bfloat16)
    tend = lax.dot_general(
        act, weight_out, (((1,), (1,)), ((), ())), preferred_element_type=jnp.float32
    ).astype(jnp.bfloat16)
    dtend = (0.5 * owner_cots.astype(jnp.float32)).astype(jnp.bfloat16)
    dact = jnp.dot(dtend, weight_out, preferred_element_type=jnp.float32)
    dpre = (dact * silu_slope(pre)).astype(jnp.bfloat16)
    adjoint = lax.dot_general(
        dpre, weight_in, (((1,), (1,)), ((), ())), preferred_element_type=jnp.float32
    ).astype(jnp.bfloat16)
    back_tend, back_adj = (
        lax.all_to_all(
            tend.reshape(owners, capacity, feats), "grp", split_axis=0, concat_axis=0, tiled=True
        ),
        lax.all_to_all(
            adjoint.reshape(owners, capacity, feats), "grp", split_axis=0, concat_axis=0, tiled=True
        ),
    )
    grad_in = lax.dot_general(
        owner_cols, dpre, (((0,), (0,)), ((), ())), preferred_element_type=jnp.float32
    )
    grad_out = lax.dot_general(
        dtend, act, (((0,), (0,)), ((), ())), preferred_element_type=jnp.float32
    )
    flat = jnp.stack([grad_in, grad_out], axis=0).reshape(-1, 128)
    summed = lax.psum_scatter(flat, ("row", "col"), scatter_dimension=0, tiled=True)
    tendency = jnp.take(back_tend.reshape(owners * capacity, feats), places, axis=0)
    column_adjoint = jnp.take(back_adj.reshape(owners * capacity, feats), places, axis=0)
    new_state = field + 0.5 * tendency.astype(jnp.float32).reshape(rows_blk, cols_blk, feats)
    return (new_state, column_adjoint.reshape(rows_blk, cols_blk, feats), summed[None])


def solution(mesh):
    in_specs = (
        P("row", ("grp", "col"), None),
        P("row", ("grp", "col")),
        P("row", ("grp", "col"), None),
        P("row", ("grp", "col"), None, None),
        P("grp", None, None),
        P("grp", None, None),
    )
    out_specs = (
        P("row", ("grp", "col"), None),
        P("row", ("grp", "col"), None),
        P("grp", ("row", "col"), None),
    )
    return jax.shard_map(local, mesh=mesh, in_specs=in_specs, out_specs=out_specs, check_vma=False)
```

profile of v0, /device:TPU:1, one launch (start us, length us, event | category | flops | bytes accessed | tf_op | source)
XLA Modules:
  0.0 243.0 jit_solution(6189310327924946195)
XLA Ops:
  7.2 1.0 convert_element_type.64
  8.3 19.3 %collective-permute-start.1 = (bf16[1,16,256]{2,1,0:T(8,128)(2,1)S(1)}, bf16[1,16,256]{2,1,0:T(8,128)(2,1)S(1)}, u32[]{:S(2)}, u32[]{:S(2)}) collective-permute-start(bf16[1,16,256]{2,1,0:T(8,128)(2,1)S(1)} %get-tuple-element.27), channel_id=1, source_target_pairs={{32,0},{64,32},{96,64},{128,96},{160,128},{192,160},{224,192},{256... | collective-permute-start | bytes 24584 | tf_op jit(solution)/shard_map/ppermute | solution.py:18
  27.5 1.9 collective-permute-start
  32.4 3.7 %collective-permute-done = bf16[1,16,256]{2,1,0:T(8,128)(2,1)S(1)} collective-permute-done((bf16[1,16,256]{2,1,0:T(8,128)(2,1)S(1)}, bf16[1,16,256]{2,1,0:T(8,128)(2,1)S(1)}, u32[]{:S(2)}, u32[]{:S(2)}) %collective-permute-start) | collective-permute-done | bytes 8224 | tf_op jit(solution)/shard_map/ppermute | solution.py:16
  36.2 4.0 %collective-permute-start.3 = (bf16[18,1,256]{2,1,0:T(2,128)(2,1)S(1)}, bf16[18,1,256]{2,1,0:T(2,128)(2,1)S(1)}, u32[]{:S(2)}, u32[]{:S(2)}) collective-permute-start(bf16[18,1,256]{2,1,0:T(2,128)(2,1)S(1)} %get-tuple-element.19), channel_id=1, source_target_pairs={{1,0},{2,1},{3,2},{4,3},{5,4},{6,5},{7,6},{8,7},{9,8},{10,9},{11,1... | collective-permute-start | bytes 27656 | tf_op jit(solution)/shard_map/ppermute | solution.py:18
  40.2 3.9 %collective-permute-start.2 = (bf16[18,1,256]{2,1,0:T(2,128)(2,1)S(1)}, bf16[18,1,256]{2,1,0:T(2,128)(2,1)S(1)}, u32[]{:S(2)}, u32[]{:S(2)}) collective-permute-start(bf16[18,1,256]{2,1,0:T(2,128)(2,1)S(1)} %get-tuple-element.18), channel_id=1, source_target_pairs={{0,1},{1,2},{2,3},{3,4},{4,5},{5,6},{6,7},{7,8},{8,9},{9,10},{10,1... | collective-permute-start | bytes 27656 | tf_op jit(solution)/shard_map/ppermute | solution.py:16
  45.1 7.7 %all-to-all-start = ((bf16[16,32,256]{2,1,0:T(8,128)(2,1)}), bf16[16,32,256]{2,1,0:T(8,128)(2,1)S(1)}, u32[]{:S(2)}, u32[]{:S(2)}) async-start(bf16[16,32,256]{2,1,0:T(8,128)(2,1)} %bitcast.4), calls=%async_computation | async-start | bytes 524288 | tf_op jit(solution)/shard_map/all_to_all | solution.py:47
  53.1 3.9 %collective-permute-start.5 = (bf16[1,16,256]{2,1,0:T(8,128)(2,1)S(1)}, bf16[1,16,256]{2,1,0:T(8,128)(2,1)S(1)}, u32[]{:S(2)}, u32[]{:S(2)}) collective-permute-start(bf16[1,16,256]{2,1,0:T(8,128)(2,1)S(1)} %get-tuple-element.25), channel_id=1, source_target_pairs={{32,0},{64,32},{96,64},{128,96},{160,128},{192,160},{224,192},{256... | collective-permute-start | bytes 24584 | tf_op jit(solution)/shard_map/ppermute | solution.py:18
  56.9 2.3 collective-permute-start.4
  60.2 4.1 %all-to-all-done = bf16[16,32,256]{2,1,0:T(8,128)(2,1)S(1)} async-done(((bf16[16,32,256]{2,1,0:T(8,128)(2,1)}), bf16[16,32,256]{2,1,0:T(8,128)(2,1)S(1)}, u32[]{:S(2)}, u32[]{:S(2)}) %all-to-all-start) | async-done | bytes 262176 | tf_op jit(solution)/shard_map/all_to_all | solution.py:47
  64.3 3.5 %all-to-all-start.2 = ((bf16[16,32,256]{2,1,0:T(8,128)(2,1)}), bf16[16,32,256]{2,1,0:T(8,128)(2,1)S(1)}, u32[]{:S(2)}, u32[]{:S(2)}) async-start(bf16[16,32,256]{2,1,0:T(8,128)(2,1)} %bitcast.12), calls=%async_computation.2 | async-start | bytes 524288 | tf_op jit(solution)/shard_map/all_to_all | solution.py:54
  68.0 3.6 %collective-permute-start.7 = (bf16[18,1,256]{2,1,0:T(2,128)(2,1)S(1)}, bf16[18,1,256]{2,1,0:T(2,128)(2,1)S(1)}, u32[]{:S(2)}, u32[]{:S(2)}) collective-permute-start(bf16[18,1,256]{2,1,0:T(2,128)(2,1)S(1)} %get-tuple-element.17), channel_id=1, source_target_pairs={{1,0},{2,1},{3,2},{4,3},{5,4},{6,5},{7,6},{8,7},{9,8},{10,9},{11,1... | collective-permute-start | bytes 27656 | tf_op jit(solution)/shard_map/ppermute | solution.py:18
  71.6 3.3 %collective-permute-start.6 = (bf16[18,1,256]{2,1,0:T(2,128)(2,1)S(1)}, bf16[18,1,256]{2,1,0:T(2,128)(2,1)S(1)}, u32[]{:S(2)}, u32[]{:S(2)}) collective-permute-start(bf16[18,1,256]{2,1,0:T(2,128)(2,1)S(1)} %get-tuple-element.16), channel_id=1, source_target_pairs={{0,1},{1,2},{2,3},{3,4},{4,5},{5,6},{6,7},{7,8},{8,9},{9,10},{10,1... | collective-permute-start | bytes 27656 | tf_op jit(solution)/shard_map/ppermute | solution.py:16
  74.9 2.0 multiply_convert_fusion.1
  81.8 1.5 reshape.96
  83.7 8.8 %collective-permute-start.9 = (bf16[1,16,256]{2,1,0:T(8,128)(2,1)S(1)}, bf16[1,16,256]{2,1,0:T(8,128)(2,1)S(1)}, u32[]{:S(2)}, u32[]{:S(2)}) collective-permute-start(bf16[1,16,256]{2,1,0:T(8,128)(2,1)S(1)} %get-tuple-element.23), channel_id=1, source_target_pairs={{32,0},{64,32},{96,64},{128,96},{160,128},{192,160},{224,192},{256... | collective-permute-start | bytes 24584 | tf_op jit(solution)/shard_map/ppermute | solution.py:18
  92.4 1.9 collective-permute-start.8
  94.4 6.7 %collective-permute-done.8 = bf16[1,16,256]{2,1,0:T(8,128)(2,1)S(1)} collective-permute-done((bf16[1,16,256]{2,1,0:T(8,128)(2,1)S(1)}, bf16[1,16,256]{2,1,0:T(8,128)(2,1)S(1)}, u32[]{:S(2)}, u32[]{:S(2)}) %collective-permute-start.8) | collective-permute-done | bytes 8224 | tf_op jit(solution)/shard_map/ppermute | solution.py:16
  101.1 5.1 %collective-permute-start.11 = (bf16[18,1,256]{2,1,0:T(2,128)(2,1)S(1)}, bf16[18,1,256]{2,1,0:T(2,128)(2,1)S(1)}, u32[]{:S(2)}, u32[]{:S(2)}) collective-permute-start(bf16[18,1,256]{2,1,0:T(2,128)(2,1)S(1)} %get-tuple-element.15), channel_id=1, source_target_pairs={{1,0},{2,1},{3,2},{4,3},{5,4},{6,5},{7,6},{8,7},{9,8},{10,9},{11,1... | collective-permute-start | bytes 27656 | tf_op jit(solution)/shard_map/ppermute | solution.py:18
  106.1 2.0 collective-permute-start.10
  109.5 1.2 convolution_convert_fusion.2
  110.7 4.8 %all-to-all-start.1 = ((bf16[16,32,256]{2,1,0:T(8,128)(2,1)}), bf16[16,32,256]{2,1,0:T(8,128)(2,1)S(1)}, u32[]{:S(2)}, u32[]{:S(2)}) async-start(bf16[16,32,256]{2,1,0:T(8,128)(2,1)} %bitcast.8), calls=%async_computation.1 | async-start | bytes 524288 | tf_op jit(solution)/shard_map/all_to_all | solution.py:85
  115.5 1.9 collective-permute-start.13
  117.4 4.3 %collective-permute-start.12 = (bf16[1,16,256]{2,1,0:T(8,128)(2,1)S(1)}, bf16[1,16,256]{2,1,0:T(8,128)(2,1)S(1)}, u32[]{:S(2)}, u32[]{:S(2)}) collective-permute-start(bf16[1,16,256]{2,1,0:T(8,128)(2,1)S(1)} %get-tuple-element.20), channel_id=1, source_target_pairs={{0,32},{32,64},{64,96},{96,128},{128,160},{160,192},{192,224},{224... | collective-permute-start | bytes 24584 | tf_op jit(solution)/shard_map/ppermute | solution.py:16
  121.7 1.2 convolution_convert_fusion
  122.9 2.4 all-to-all-done.1
  125.2 5.2 %all-to-all-start.3 = ((bf16[16,32,256]{2,1,0:T(8,128)(2,1)}), bf16[16,32,256]{2,1,0:T(8,128)(2,1)S(1)}, u32[]{:S(2)}, u32[]{:S(2)}) async-start(bf16[16,32,256]{2,1,0:T(8,128)(2,1)} %bitcast.14), calls=%async_computation.3 | async-start | bytes 524288 | tf_op jit(solution)/shard_map/all_to_all | solution.py:88
  130.5 6.6 %collective-permute-start.15 = (bf16[18,1,256]{2,1,0:T(2,128)(2,1)S(1)}, bf16[18,1,256]{2,1,0:T(2,128)(2,1)S(1)}, u32[]{:S(2)}, u32[]{:S(2)}) collective-permute-start(bf16[18,1,256]{2,1,0:T(2,128)(2,1)S(1)} %get-tuple-element.13), channel_id=1, source_target_pairs={{1,0},{2,1},{3,2},{4,3},{5,4},{6,5},{7,6},{8,7},{9,8},{10,9},{11,1... | collective-permute-start | bytes 27656 | tf_op jit(solution)/shard_map/ppermute | solution.py:18
  137.2 3.4 %collective-permute-start.14 = (bf16[18,1,256]{2,1,0:T(2,128)(2,1)S(1)}, bf16[18,1,256]{2,1,0:T(2,128)(2,1)S(1)}, u32[]{:S(2)}, u32[]{:S(2)}) collective-permute-start(bf16[18,1,256]{2,1,0:T(2,128)(2,1)S(1)} %get-tuple-element.12), channel_id=1, source_target_pairs={{0,1},{1,2},{2,3},{3,4},{4,5},{5,6},{6,7},{7,8},{8,9},{9,10},{10,1... | collective-permute-start | bytes 27656 | tf_op jit(solution)/shard_map/ppermute | solution.py:16
  141.6 1.2 gather_fusion
  142.7 1.2 gather_fusion.1
  145.6 90.6 %reduce-scatter.2.cloned.1.call-done = f32[64,128]{1,0:T(8,128)} async-done(((f32[4096,128]{1,0:T(8,128)}), f32[64,128]{1,0:T(8,128)}) %reduce-scatter.2.cloned.1.call-update) | async-done | bytes 32784 | tf_op jit(solution)/shard_map/reduce_scatter | solution.py:99
  (74 shorter events, 14.3 us)
Async XLA Ops:
  7.2 67.7 %copy-start = (bf16[1,256,1024]{2,1,0:T(8,128)(2,1)S(1)}, bf16[1,256,1024]{2,1,0:T(8,128)(2,1)}, u32[]{:S(2)}) copy-start(bf16[1,256,1024]{2,1,0:T(8,128)(2,1)} %param.12) | copy-start | bytes 1572868
  7.2 45.7 %copy-start.5 = (f32[16,16,256]{2,1,0:T(8,128)S(1)}, f32[16,16,256]{2,1,0:T(8,128)}, u32[]{:S(2)}) copy-start(f32[16,16,256]{2,1,0:T(8,128)} %param.8) | copy-start | bytes 786436
  7.2 45.7 %copy-start.6 = (f32[16,16]{1,0:T(8,128)S(1)}, f32[16,16]{1,0:T(8,128)}, u32[]{:S(2)}) copy-start(f32[16,16]{1,0:T(8,128)} %param.9) | copy-start | bytes 3076
  7.2 52.1 %copy-start.7 = (bf16[16,16,256]{2,1,0:T(8,128)(2,1)S(1)}, bf16[16,16,256]{2,1,0:T(8,128)(2,1)}, u32[]{:S(2)}) copy-start(bf16[16,16,256]{2,1,0:T(8,128)(2,1)} %param.10) | copy-start | bytes 393220
  8.3 24.1 %collective-permute-start.1 = (bf16[1,16,256]{2,1,0:T(8,128)(2,1)S(1)}, bf16[1,16,256]{2,1,0:T(8,128)(2,1)S(1)}, u32[]{:S(2)}, u32[]{:S(2)}) collective-permute-start(bf16[1,16,256]{2,1,0:T(8,128)(2,1)S(1)} %get-tuple-element.27), channel_id=1, source_target_pairs={{32,0},{64,32},{96,64},{128,96},{160,128},{192,160},{224,192},{256... | collective-permute-start | bytes 24584 | tf_op jit(solution)/shard_map/ppermute | solution.py:18
  27.5 8.6 %collective-permute-start = (bf16[1,16,256]{2,1,0:T(8,128)(2,1)S(1)}, bf16[1,16,256]{2,1,0:T(8,128)(2,1)S(1)}, u32[]{:S(2)}, u32[]{:S(2)}) collective-permute-start(bf16[1,16,256]{2,1,0:T(8,128)(2,1)S(1)} %get-tuple-element.26), channel_id=1, source_target_pairs={{0,32},{32,64},{64,96},{96,128},{128,160},{160,192},{192,224},{224... | collective-permute-start | bytes 24584 | tf_op jit(solution)/shard_map/ppermute | solution.py:16
  36.2 16.6 %collective-permute-start.3 = (bf16[18,1,256]{2,1,0:T(2,128)(2,1)S(1)}, bf16[18,1,256]{2,1,0:T(2,128)(2,1)S(1)}, u32[]{:S(2)}, u32[]{:S(2)}) collective-permute-start(bf16[18,1,256]{2,1,0:T(2,128)(2,1)S(1)} %get-tuple-element.19), channel_id=1, source_target_pairs={{1,0},{2,1},{3,2},{4,3},{5,4},{6,5},{7,6},{8,7},{9,8},{10,9},{11,1... | collective-permute-start | bytes 27656 | tf_op jit(solution)/shard_map/ppermute | solution.py:18
  40.2 12.6 %collective-permute-start.2 = (bf16[18,1,256]{2,1,0:T(2,128)(2,1)S(1)}, bf16[18,1,256]{2,1,0:T(2,128)(2,1)S(1)}, u32[]{:S(2)}, u32[]{:S(2)}) collective-permute-start(bf16[18,1,256]{2,1,0:T(2,128)(2,1)S(1)} %get-tuple-element.18), channel_id=1, source_target_pairs={{0,1},{1,2},{2,3},{3,4},{4,5},{5,6},{6,7},{7,8},{8,9},{9,10},{10,1... | collective-permute-start | bytes 27656 | tf_op jit(solution)/shard_map/ppermute | solution.py:16
  45.1 19.3 %all-to-all-start = ((bf16[16,32,256]{2,1,0:T(8,128)(2,1)}), bf16[16,32,256]{2,1,0:T(8,128)(2,1)S(1)}, u32[]{:S(2)}, u32[]{:S(2)}) async-start(bf16[16,32,256]{2,1,0:T(8,128)(2,1)} %bitcast.4), calls=%async_computation | async-start | bytes 524288 | tf_op jit(solution)/shard_map/all_to_all | solution.py:47
  53.1 14.8 %collective-permute-start.5 = (bf16[1,16,256]{2,1,0:T(8,128)(2,1)S(1)}, bf16[1,16,256]{2,1,0:T(8,128)(2,1)S(1)}, u32[]{:S(2)}, u32[]{:S(2)}) collective-permute-start(bf16[1,16,256]{2,1,0:T(8,128)(2,1)S(1)} %get-tuple-element.25), channel_id=1, source_target_pairs={{32,0},{64,32},{96,64},{128,96},{160,128},{192,160},{224,192},{256... | collective-permute-start | bytes 24584 | tf_op jit(solution)/shard_map/ppermute | solution.py:18
  56.9 11.0 %collective-permute-start.4 = (bf16[1,16,256]{2,1,0:T(8,128)(2,1)S(1)}, bf16[1,16,256]{2,1,0:T(8,128)(2,1)S(1)}, u32[]{:S(2)}, u32[]{:S(2)}) collective-permute-start(bf16[1,16,256]{2,1,0:T(8,128)(2,1)S(1)} %get-tuple-element.24), channel_id=1, source_target_pairs={{0,32},{32,64},{64,96},{96,128},{128,160},{160,192},{192,224},{224... | collective-permute-start | bytes 24584 | tf_op jit(solution)/shard_map/ppermute | solution.py:16
  64.3 13.2 %all-to-all-start.2 = ((bf16[16,32,256]{2,1,0:T(8,128)(2,1)}), bf16[16,32,256]{2,1,0:T(8,128)(2,1)S(1)}, u32[]{:S(2)}, u32[]{:S(2)}) async-start(bf16[16,32,256]{2,1,0:T(8,128)(2,1)} %bitcast.12), calls=%async_computation.2 | async-start | bytes 524288 | tf_op jit(solution)/shard_map/all_to_all | solution.py:54
  67.9 168.3 %reduce-scatter.2.cloned.1.call-start = ((), (), s32[]{:S(2)}) async-start(), calls=%async_computation.5 | async-start | bytes 2129920 | tf_op jit(solution)/shard_map/reduce_scatter | solution.py:99
  68.0 15.4 %collective-permute-start.7 = (bf16[18,1,256]{2,1,0:T(2,128)(2,1)S(1)}, bf16[18,1,256]{2,1,0:T(2,128)(2,1)S(1)}, u32[]{:S(2)}, u32[]{:S(2)}) collective-permute-start(bf16[18,1,256]{2,1,0:T(2,128)(2,1)S(1)} %get-tuple-element.17), channel_id=1, source_target_pairs={{1,0},{2,1},{3,2},{4,3},{5,4},{6,5},{7,6},{8,7},{9,8},{10,9},{11,1... | collective-permute-start | bytes 27656 | tf_op jit(solution)/shard_map/ppermute | solution.py:18
  71.6 11.8 %collective-permute-start.6 = (bf16[18,1,256]{2,1,0:T(2,128)(2,1)S(1)}, bf16[18,1,256]{2,1,0:T(2,128)(2,1)S(1)}, u32[]{:S(2)}, u32[]{:S(2)}) collective-permute-start(bf16[18,1,256]{2,1,0:T(2,128)(2,1)S(1)} %get-tuple-element.16), channel_id=1, source_target_pairs={{0,1},{1,2},{2,3},{3,4},{4,5},{5,6},{6,7},{7,8},{8,9},{9,10},{10,1... | collective-permute-start | bytes 27656 | tf_op jit(solution)/shard_map/ppermute | solution.py:16
  76.9 1.2 copy-start.3
  77.6 1.0 copy-start.8
  77.6 1.8 copy-start.10
  80.2 1.0 copy-start.1
  83.5 25.9 %copy-start.4 = (bf16[512,1024]{1,0:T(8,128)(2,1)S(1)}, bf16[512,1024]{1,0:T(8,128)(2,1)}, u32[]{:S(2)}) copy-start(bf16[512,1024]{1,0:T(8,128)(2,1)} %copy-done.3) | copy-start | bytes 3145732
  83.5 25.9 %copy-start.9 = (bf16[1,256,1024]{2,1,0:T(8,128)(2,1)S(1)}, bf16[1,256,1024]{2,1,0:T(8,128)(2,1)}, u32[]{:S(2)}) copy-start(bf16[1,256,1024]{2,1,0:T(8,128)(2,1)} %param.13) | copy-start | bytes 1572868
  83.7 10.7 %collective-permute-start.9 = (bf16[1,16,256]{2,1,0:T(8,128)(2,1)S(1)}, bf16[1,16,256]{2,1,0:T(8,128)(2,1)S(1)}, u32[]{:S(2)}, u32[]{:S(2)}) collective-permute-start(bf16[1,16,256]{2,1,0:T(8,128)(2,1)S(1)} %get-tuple-element.23), channel_id=1, source_target_pairs={{32,0},{64,32},{96,64},{128,96},{160,128},{192,160},{224,192},{256... | collective-permute-start | bytes 24584 | tf_op jit(solution)/shard_map/ppermute | solution.py:18
  92.4 8.6 %collective-permute-start.8 = (bf16[1,16,256]{2,1,0:T(8,128)(2,1)S(1)}, bf16[1,16,256]{2,1,0:T(8,128)(2,1)S(1)}, u32[]{:S(2)}, u32[]{:S(2)}) collective-permute-start(bf16[1,16,256]{2,1,0:T(8,128)(2,1)S(1)} %get-tuple-element.22), channel_id=1, source_target_pairs={{0,32},{32,64},{64,96},{96,128},{128,160},{160,192},{192,224},{224... | collective-permute-start | bytes 24584 | tf_op jit(solution)/shard_map/ppermute | solution.py:16
  101.1 7.1 %collective-permute-start.11 = (bf16[18,1,256]{2,1,0:T(2,128)(2,1)S(1)}, bf16[18,1,256]{2,1,0:T(2,128)(2,1)S(1)}, u32[]{:S(2)}, u32[]{:S(2)}) collective-permute-start(bf16[18,1,256]{2,1,0:T(2,128)(2,1)S(1)} %get-tuple-element.15), channel_id=1, source_target_pairs={{1,0},{2,1},{3,2},{4,3},{5,4},{6,5},{7,6},{8,7},{9,8},{10,9},{11,1... | collective-permute-start | bytes 27656 | tf_op jit(solution)/shard_map/ppermute | solution.py:18
  106.1 3.1 %collective-permute-start.10 = (bf16[18,1,256]{2,1,0:T(2,128)(2,1)S(1)}, bf16[18,1,256]{2,1,0:T(2,128)(2,1)S(1)}, u32[]{:S(2)}, u32[]{:S(2)}) collective-permute-start(bf16[18,1,256]{2,1,0:T(2,128)(2,1)S(1)} %get-tuple-element.14), channel_id=1, source_target_pairs={{0,1},{1,2},{2,3},{3,4},{4,5},{5,6},{6,7},{7,8},{8,9},{9,10},{10,1... | collective-permute-start | bytes 27656 | tf_op jit(solution)/shard_map/ppermute | solution.py:16
  109.3 12.4 %copy-start.2 = (bf16[512,1024]{1,0:T(8,128)(2,1)S(1)}, bf16[512,1024]{1,0:T(8,128)(2,1)}, u32[]{:S(2)}) copy-start(bf16[512,1024]{1,0:T(8,128)(2,1)} %copy-done.1) | copy-start | bytes 3145732
  110.7 14.6 %all-to-all-start.1 = ((bf16[16,32,256]{2,1,0:T(8,128)(2,1)}), bf16[16,32,256]{2,1,0:T(8,128)(2,1)S(1)}, u32[]{:S(2)}, u32[]{:S(2)}) async-start(bf16[16,32,256]{2,1,0:T(8,128)(2,1)} %bitcast.8), calls=%async_computation.1 | async-start | bytes 524288 | tf_op jit(solution)/shard_map/all_to_all | solution.py:85
  115.5 15.0 %collective-permute-start.13 = (bf16[1,16,256]{2,1,0:T(8,128)(2,1)S(1)}, bf16[1,16,256]{2,1,0:T(8,128)(2,1)S(1)}, u32[]{:S(2)}, u32[]{:S(2)}) collective-permute-start(bf16[1,16,256]{2,1,0:T(8,128)(2,1)S(1)} %get-tuple-element.21), channel_id=1, source_target_pairs={{32,0},{64,32},{96,64},{128,96},{160,128},{192,160},{224,192},{256... | collective-permute-start | bytes 24584 | tf_op jit(solution)/shard_map/ppermute | solution.py:18
  117.4 13.0 %collective-permute-start.12 = (bf16[1,16,256]{2,1,0:T(8,128)(2,1)S(1)}, bf16[1,16,256]{2,1,0:T(8,128)(2,1)S(1)}, u32[]{:S(2)}, u32[]{:S(2)}) collective-permute-start(bf16[1,16,256]{2,1,0:T(8,128)(2,1)S(1)} %get-tuple-element.20), channel_id=1, source_target_pairs={{0,32},{32,64},{64,96},{96,128},{128,160},{160,192},{192,224},{224... | collective-permute-start | bytes 24584 | tf_op jit(solution)/shard_map/ppermute | solution.py:16
  125.2 17.5 %all-to-all-start.3 = ((bf16[16,32,256]{2,1,0:T(8,128)(2,1)}), bf16[16,32,256]{2,1,0:T(8,128)(2,1)S(1)}, u32[]{:S(2)}, u32[]{:S(2)}) async-start(bf16[16,32,256]{2,1,0:T(8,128)(2,1)} %bitcast.14), calls=%async_computation.3 | async-start | bytes 524288 | tf_op jit(solution)/shard_map/all_to_all | solution.py:88
  130.5 10.1 %collective-permute-start.15 = (bf16[18,1,256]{2,1,0:T(2,128)(2,1)S(1)}, bf16[18,1,256]{2,1,0:T(2,128)(2,1)S(1)}, u32[]{:S(2)}, u32[]{:S(2)}) collective-permute-start(bf16[18,1,256]{2,1,0:T(2,128)(2,1)S(1)} %get-tuple-element.13), channel_id=1, source_target_pairs={{1,0},{2,1},{3,2},{4,3},{5,4},{6,5},{7,6},{8,7},{9,8},{10,9},{11,1... | collective-permute-start | bytes 27656 | tf_op jit(solution)/shard_map/ppermute | solution.py:18
  137.2 4.3 %collective-permute-start.14 = (bf16[18,1,256]{2,1,0:T(2,128)(2,1)S(1)}, bf16[18,1,256]{2,1,0:T(2,128)(2,1)S(1)}, u32[]{:S(2)}, u32[]{:S(2)}) collective-permute-start(bf16[18,1,256]{2,1,0:T(2,128)(2,1)S(1)} %get-tuple-element.12), channel_id=1, source_target_pairs={{0,1},{1,2},{2,3},{3,4},{4,5},{5,6},{6,7},{7,8},{8,9},{9,10},{10,1... | collective-permute-start | bytes 27656 | tf_op jit(solution)/shard_map/ppermute | solution.py:16
Sparse Core Ops, SparseCore 0:
  83.5 152.6 reduce-scatter.1
where the time goes:
time: 248 us; the launch traced here: 243 us
  waiting for transfers between devices  110 us (44%)
  starting transfers between devices  97.5 us (39%)
  between operations  14.6 us (6%)
  matrix products  7.98 us (3%)
  other arithmetic  6.62 us (3%)
  local copies, waits for them, and re-layouts  6.28 us (3%)
    reduce_scatter x1, waiting for transfers between devices, local(): lax.psum_scatter(flat, ('row', 'col'), scatter_dimension=0, tiled=True)  90.6 us
    ppermute x8, starting transfers between devices, padded_2(): lax.ppermute(head, axis, [((i + 1) % count, i) for i in range(count)])  53.1 us
    ppermute x8, starting transfers between devices, padded_2(): lax.ppermute(tail, axis, [(i, (i + 1) % count) for i in range(count)])  23.1 us
    ppermute x8, waiting for transfers between devices, padded_2(): lax.ppermute(tail, axis, [(i, (i + 1) % count) for i in range(count)])  12.3 us
    all_to_all x1, starting transfers between devices, local(): lax.all_to_all(packed_cols.reshape(owners, capacity, feats), 'grp', split...  7.74 us
    all_to_all x1, starting transfers between devices, local(): lax.all_to_all(adjoint.reshape(owners, capacity, feats), 'grp', split_axi...  5.19 us
  transfers between devices with their start and end apart: 21, of which 8 were waited for; matrix products, arithmetic and copies ran while one was open for 7% of the time, Pallas kernels for 0%

commit v1 on v0

v1 whole, which is shorter than its diff:
```python
import jax
import jax.numpy as jnp
from jax import lax
from jax.experimental import pallas as pl
from jax.experimental.pallas import tpu as pltpu
from jax.sharding import PartitionSpec as P

F32, BF16, I32 = jnp.float32, jnp.bfloat16, jnp.int32
MESH = pl.DeviceIdType.MESH

STEPS = 4
SIDE = 16
FEATS = 256
HID = 1024
CAP = 32
ROWS, BLOCKS = 32, 32
NX, NZ = 8, 4
NY, NL = 8, 2
SLOTS = NY * NL
COLUMNS = SIDE * SIDE
WIDE = FEATS + 128
XF = 640
TN = 256

OFFSETS = sorted(
    ((dy, dl) for dy in range(NY) for dl in range(NL)),
    key=lambda o: 4 * ((4 - min(o[0], 8 - o[0])) % 4) + 2 * (o[0] >= 4) + o[1],
)
SENDING = [2, 3, 1] + list(range(4, SLOTS))
SIDES = [(0, 1), (0, -1), (1, 0), (-1, 0), (1, 1), (1, -1), (-1, 1), (-1, -1)]
FAR_X = [4, 3, 5, 2, 6, 1, 7]
FAR_Z = [2, 1, 3]


def iota(shape, dim):
    return lax.broadcasted_iota(I32, shape, dim)


def kernel(
    state_ref,
    rate_ref,
    cot_ref,
    dest_ref,
    win_hbm,
    wout_hbm,
    new_ref,
    adj_ref,
    grad_ref,
    win,
    wout,
    send,
    recv,
    back,
    home,
    places_ref,
    act_ref,
    dpre_ref,
    edge,
    halo,
    field_a,
    field_b,
    rates,
    grads,
    pair,
    half,
    x1,
    z1,
    sum_x,
    out_x,
    z2,
    sum_z,
    out_z,
    x2,
    w_sem,
    fwd_send,
    fwd_recv,
    back_send,
    back_recv,
    edge_send,
    edge_recv,
    pair_send,
    pair_recv,
    x1_send,
    x1_recv,
    z1_send,
    z1_recv,
    x2_send,
    x2_recv,
    z2_send,
    z2_recv,
):
    row, grp, col = lax.axis_index("row"), lax.axis_index("grp"), lax.axis_index("col")
    x, z = row // NZ, row % NZ
    y, l = grp // NL, grp % NL
    block = grp * 2 + col

    def at_expert(dy, dl):
        return {"row": row, "grp": ((y + dy) % NY) * NL + (l + dl) % NL, "col": col}

    def at_source(dy, dl):
        return {"row": row, "grp": ((y + NY - dy) % NY) * NL + (l + dl) % NL, "col": col}

    def at_side(di, dj):
        there = (block + dj + BLOCKS) % BLOCKS
        return {"row": (row + di + ROWS) % ROWS, "grp": there // 2, "col": there % 2}

    def at_x(dx):
        return {"row": ((x + dx) % NX) * NZ + z, "grp": grp, "col": col}

    def at_z(dz):
        return {"row": x * NZ + (z + dz) % NZ, "grp": grp, "col": col}

    partner = {"row": row, "grp": grp, "col": 1 - col}

    barrier = pltpu.get_barrier_semaphore()
    greeted = (
        [at_expert(*OFFSETS[t]) for t in SENDING]
        + [at_side(*o) for o in SIDES]
        + [at_x(dx) for dx in FAR_X]
        + [at_z(dz) for dz in FAR_Z]
        + [partner]
    )
    for there in greeted:
        pl.semaphore_signal(barrier, inc=1, device_id=there, device_id_type=MESH)

    def remote(src, dst, sent, came, there):
        return pltpu.make_async_remote_copy(
            src_ref=src, dst_ref=dst, send_sem=sent, recv_sem=came, device_id=there, device_id_type=MESH
        )

    w_copies = [
        pltpu.make_async_copy(win_hbm, win, w_sem.at[0]),
        pltpu.make_async_copy(wout_hbm, wout, w_sem.at[1]),
    ]
    for copy in w_copies:
        copy.start()

    dest = dest_ref[...]
    dy = ((dest >> 1) - y) & (NY - 1)
    dl = (dest & 1) ^ l
    slot = ((4 - jnp.minimum(dy, NY - dy)) & 3) * 4 + jnp.where(dy >= 4, 2, 0) + dl
    chosen = jnp.where(iota((SLOTS, COLUMNS), 0) == slot, 1.0, 0.0)
    upto = jnp.where(
        iota((COLUMNS, COLUMNS), 0) <= iota((COLUMNS, COLUMNS), 1), 1.0, 0.0
    ).astype(BF16)
    ranks = jnp.dot(chosen.astype(BF16), upto, preferred_element_type=F32)
    rank = jnp.sum(chosen * ranks, axis=0, keepdims=True) - 1.0
    places = slot.astype(F32) * CAP + rank
    places_ref[...] = places
    placing = jnp.where(
        iota((SLOTS * CAP, COLUMNS), 0) == places.astype(I32), 1.0, 0.0
    ).astype(BF16)
    cells = state_ref[...].astype(BF16)
    packed = jnp.dot(placing, cells.reshape(COLUMNS, FEATS), preferred_element_type=F32)
    packed = packed.astype(BF16).reshape(SLOTS, CAP, FEATS)
    send[:, :, 0:FEATS] = packed
    recv[0, :, 0:FEATS] = packed[0]
    packed = 0.5 * jnp.dot(
        placing, cot_ref[...].reshape(COLUMNS, FEATS), preferred_element_type=F32
    )
    packed = packed.astype(BF16).reshape(SLOTS, CAP, FEATS)
    send[:, :, FEATS:] = packed
    recv[0, :, FEATS:] = packed[0]

    edge[:, :, :, 0:FEATS] = cells.reshape(SIDE, 2, 8, FEATS)
    diagonal = iota((SIDE, SIDE), 0) == iota((SIDE, SIDE), 1)
    for i in range(SIDE):
        line = jnp.broadcast_to(rate_ref[i : i + 1, :], (SIDE, SIDE))
        line = jnp.sum(jnp.where(diagonal, line, 0.0), axis=1, keepdims=True)
        line = jnp.broadcast_to(line, (SIDE, 128))
        rates[4 + i, 8 : 8 + SIDE, :] = line
        edge[i, :, :, FEATS:] = line.astype(BF16).reshape(2, 8, 128)

    pl.semaphore_wait(barrier, len(greeted))

    fwd = {
        t: remote(send.at[t], recv.at[t], fwd_send.at[t], fwd_recv.at[t], at_expert(*OFFSETS[t]))
        for t in SENDING
    }
    for t in SENDING:
        fwd[t].start()

    span = {-1: (slice(0, 4), slice(20, 24)), 1: (slice(12, 16), slice(0, 4)), 0: (slice(0, 16), slice(4, 20))}
    tile = {-1: (slice(0, 1), slice(3, 4)), 1: (slice(1, 2), slice(0, 1)), 0: (slice(0, 2), slice(1, 3))}
    edges = [
        remote(
            edge.at[span[di][0], tile[dj][0]],
            halo.at[span[di][1], tile[dj][1]],
            edge_send.at[n],
            edge_recv.at[n],
            at_side(di, dj),
        )
        for n, (di, dj) in enumerate(SIDES)
    ]
    for copy in edges:
        copy.start()

    for copy in w_copies:
        copy.wait()

    homeward = {
        t: remote(back.at[t], home.at[t], back_send.at[t], back_recv.at[t], at_source(*OFFSETS[t]))
        for t in SENDING
    }
    for g in range(4):
        for t in range(4 * g, 4 * g + 4):
            if t:
                fwd[t].wait_recv()
        lines = slice(128 * g, 128 * g + 128)
        came = recv[4 * g : 4 * g + 4].reshape(128, 2 * FEATS)
        columns, dtend = came[:, 0:FEATS], came[:, FEATS:]
        for h in range(0, HID, TN):
            pre = jnp.dot(columns, win[:, h : h + TN], preferred_element_type=F32)
            dact = jnp.dot(dtend, wout[:, h : h + TN], preferred_element_type=F32)
            sigma = 1.0 / (1.0 + jnp.exp(-pre))
            act_ref[lines, h : h + TN] = (pre * sigma).astype(BF16)
            slope = sigma * (1.0 + pre * (1.0 - sigma))
            dpre_ref[lines, h : h + TN] = (dact * slope).astype(BF16)
        across = (((1,), (1,)), ((), ()))
        tend = lax.dot_general(act_ref[lines, :], wout[...], across, preferred_element_type=F32)
        adjoint = lax.dot_general(dpre_ref[lines, :], win[...], across, preferred_element_type=F32)
        tend = tend.astype(BF16).reshape(4, CAP, FEATS)
        adjoint = adjoint.astype(BF16).reshape(4, CAP, FEATS)
        back[4 * g : 4 * g + 4, :, 0:FEATS] = tend
        back[4 * g : 4 * g + 4, :, FEATS:] = adjoint
        if g == 0:
            home[0, :, 0:FEATS] = tend[0]
            home[0, :, FEATS:] = adjoint[0]
        for t in range(4 * g, 4 * g + 4):
            if t:
                homeward[t].start()

    pairs = []
    for n, (first, hidden) in enumerate(((FEATS, act_ref), (0, dpre_ref))):
        left = recv[:, :, first : first + FEATS].reshape(SLOTS * CAP, FEATS)
        out = slice(16 - 16 * n, 32 - 16 * n)
        for h in range(0, HID, TN):
            part = lax.dot_general(
                left, hidden[:, h : h + TN], (((0,), (0,)), ((), ())), preferred_element_type=F32
            )
            grads[out, :, :, h : h + TN] = part.reshape(16, 2, 8, TN)
        copy = remote(grads.at[out, 1 - col], pair.at[out], pair_send.at[n], pair_recv.at[n], partner)
        copy.start()
        pairs.append(copy)
    for n, copy in enumerate(pairs):
        copy.wait_recv()
        out = slice(16 - 16 * n, 32 - 16 * n)
        both = grads[out, col] + pair[out]
        half[4 - 4 * n : 8 - 4 * n] = both.astype(BF16).reshape(4, NZ, 8, HID)

    first_x = [
        remote(
            half.at[(x + dx) % NX, :, :, 0:XF], x1.at[dx], x1_send.at[dx], x1_recv.at[dx], at_x(dx)
        )
        for dx in FAR_X
    ]
    first_z = [
        remote(
            half.at[:, (z + dz) % NZ, :, XF:], z1.at[dz], z1_send.at[dz], z1_recv.at[dz], at_z(dz)
        )
        for dz in FAR_Z
    ]
    for copy in first_x + first_z:
        copy.start()

    for copy in edges:
        copy.wait_recv()
    for top in (0, 20):
        cells = halo[top : top + 4].astype(F32).reshape(4, 32, WIDE)
        field_a[top : top + 4] = cells[:, :, 0:FEATS]
        rates[top : top + 4] = cells[:, :, FEATS:]
    for t in (0, 3):
        cells = halo[4:20, t].astype(F32)
        field_a[4:20, 8 * t : 8 * t + 8] = cells[:, :, 0:FEATS]
        rates[4:20, 8 * t : 8 * t + 8] = cells[:, :, FEATS:]
    field_a[4:20, 8:24] = state_ref[...]
    old, new = field_a, field_b
    for step in range(1, STEPS + 1):

        def advance(n, carry, old=old, new=new, step=step):
            i = step + 2 * n
            here = old[pl.ds(i, 2)]
            beside = old[pl.ds(i - 1, 2)] + old[pl.ds(i + 1, 2)]
            beside = beside + pltpu.roll(here, 1, 1) + pltpu.roll(here, 31, 1)
            pace = rates[pl.ds(i, 2)]
            pace = jnp.concatenate([pace, pace], axis=2)
            new[pl.ds(i, 2)] = here + pace * (beside - 4.0 * here)
            return carry

        lax.fori_loop(0, 12 - step, advance, 0)
        old, new = new, old

    for copy in first_x:
        copy.wait_recv()
    total = half[x, :, :, 0:XF].astype(F32)
    for dx in range(1, NX):
        total = total + x1[dx].astype(F32)
    sum_x[...] = total
    out_x[...] = total.astype(BF16)
    last_z = [
        remote(out_x.at[(z + dz) % NZ], z2.at[dz], z2_send.at[dz], z2_recv.at[dz], at_z(dz)) for dz in FAR_Z
    ]
    for copy in last_z:
        copy.start()
    for copy in first_z:
        copy.wait_recv()
    total = half[:, z, :, XF:].astype(F32)
    for dz in range(1, NZ):
        total = total + z1[dz].astype(F32)
    sum_z[...] = total
    out_z[...] = total.astype(BF16)
    last_x = [
        remote(out_z.at[(x + dx) % NX], x2.at[dx], x2_send.at[dx], x2_recv.at[dx], at_x(dx)) for dx in FAR_X
    ]
    for copy in last_x:
        copy.start()

    for t in SENDING:
        homeward[t].wait_recv()
    square = iota((COLUMNS, COLUMNS), 0) == iota((COLUMNS, COLUMNS), 1)
    tall = jnp.where(square, jnp.broadcast_to(places_ref[...], (COLUMNS, COLUMNS)), 0.0)
    tall = jnp.sum(tall, axis=1, keepdims=True).astype(I32)
    picking = jnp.where(iota((COLUMNS, SLOTS * CAP), 1) == tall, 1.0, 0.0).astype(BF16)
    tend = jnp.dot(
        picking, home[:, :, 0:FEATS].reshape(SLOTS * CAP, FEATS), preferred_element_type=F32
    )
    new_ref[...] = old[4:20, 8:24] + 0.5 * tend.reshape(SIDE, SIDE, FEATS)
    adjoint = jnp.dot(
        picking, home[:, :, FEATS:].reshape(SLOTS * CAP, FEATS), preferred_element_type=F32
    )
    adj_ref[...] = adjoint.astype(BF16).reshape(SIDE, SIDE, FEATS)

    for copy in last_z:
        copy.wait_recv()
    total = sum_x[z]
    for dz in range(1, NZ):
        total = total + z2[dz].astype(F32)
    for h in range(0, XF, 128):
        grad_ref[pl.ds(h // 128, 8, stride=8), :] = total[:, h : h + 128]
    for copy in last_x:
        copy.wait_recv()
    total = sum_z[x]
    for dx in range(1, NX):
        total = total + x2[dx].astype(F32)
    for h in range(XF, HID, 128):
        grad_ref[pl.ds(h // 128, 8, stride=8), :] = total[:, h - XF : h - XF + 128]

    for t in SENDING:
        fwd[t].wait_send()
        homeward[t].wait_send()
    for copy in edges + pairs + first_x + first_z + last_x + last_z:
        copy.wait_send()


def local(state, rate, cotangent, dest, w_in, w_out):
    vmem = pl.BlockSpec(memory_space=pltpu.VMEM)
    hbm = pl.BlockSpec(memory_space=pl.ANY)
    sems = pltpu.SemaphoreType.DMA
    new_state, adjoint, grads = pl.pallas_call(
        kernel,
        out_shape=(
            jax.ShapeDtypeStruct((SIDE, SIDE, FEATS), F32),
            jax.ShapeDtypeStruct((SIDE, SIDE, FEATS), BF16),
            jax.ShapeDtypeStruct((HID // 128 * 8, 128), F32),
        ),
        in_specs=[vmem, vmem, vmem, vmem, hbm, hbm],
        out_specs=(vmem, vmem, vmem),
        scratch_shapes=[
            pltpu.VMEM((FEATS, HID), BF16),
            pltpu.VMEM((FEATS, HID), BF16),
            pltpu.VMEM((SLOTS, CAP, 2 * FEATS), BF16),
            pltpu.VMEM((SLOTS, CAP, 2 * FEATS), BF16),
            pltpu.VMEM((SLOTS, CAP, 2 * FEATS), BF16),
            pltpu.VMEM((SLOTS, CAP, 2 * FEATS), BF16),
            pltpu.VMEM((1, COLUMNS), F32),
            pltpu.VMEM((SLOTS * CAP, HID), BF16),
            pltpu.VMEM((SLOTS * CAP, HID), BF16),
            pltpu.VMEM((SIDE, 2, 8, WIDE), BF16),
            pltpu.VMEM((24, 4, 8, WIDE), BF16),
            pltpu.VMEM((24, 32, FEATS), F32),
            pltpu.VMEM((24, 32, FEATS), F32),
            pltpu.VMEM((24, 32, 128), F32),
            pltpu.VMEM((32, 2, 8, HID), F32),
            pltpu.VMEM((32, 8, HID), F32),
            pltpu.VMEM((NX, NZ, 8, HID), BF16),
            pltpu.VMEM((NX, NZ, 8, XF), BF16),
            pltpu.VMEM((NZ, NX, 8, HID - XF), BF16),
            pltpu.VMEM((NZ, 8, XF), F32),
            pltpu.VMEM((NZ, 8, XF), BF16),
            pltpu.VMEM((NZ, 8, XF), BF16),
            pltpu.VMEM((NX, 8, HID - XF), F32),
            pltpu.VMEM((NX, 8, HID - XF), BF16),
            pltpu.VMEM((NX, 8, HID - XF), BF16),
            sems((2,)),
            sems((SLOTS,)),
            sems((SLOTS,)),
            sems((SLOTS,)),
            sems((SLOTS,)),
            sems((8,)),
            sems((8,)),
            sems((2,)),
            sems((2,)),
            sems((NX,)),
            sems((NX,)),
            sems((NZ,)),
            sems((NZ,)),
            sems((NX,)),
            sems((NX,)),
            sems((NZ,)),
            sems((NZ,)),
        ],
        compiler_params=pltpu.CompilerParams(collective_id=0, has_side_effects=True),
        name="window",
    )(state, rate, cotangent, dest.reshape(1, COLUMNS), w_in[0], w_out[0])
    return new_state, adjoint, grads[None]


def solution(mesh):
    in_specs = (
        P("row", ("grp", "col"), None),
        P("row", ("grp", "col")),
        P("row", ("grp", "col"), None),
        P("row", ("grp", "col"), None, None),
        P("grp", None, None),
        P("grp", None, None),
    )
    out_specs = (
        P("row", ("grp", "col"), None),
        P("row", ("grp", "col"), None),
        P("grp", ("row", "col"), None),
    )
    return jax.shard_map(local, mesh=mesh, in_specs=in_specs, out_specs=out_specs, check_vma=False)
```

time: 248 us -> 62.7 us (0.25); the launches traced: 243 us -> 62.5 us
  waiting for transfers between devices: 110 us -> 0 us
  starting transfers between devices: 97.5 us -> 0 us
  Pallas kernels: 0 us -> 58.7 us
  between operations: 14.6 us -> 0.65 us
  matrix products: 7.98 us -> 0 us
  other arithmetic: 6.62 us -> 0 us
  local copies, waits for them, and re-layouts: 6.28 us -> 3.08 us
    reduce_scatter x1 -> x0, waiting for transfers between devices: 90.6 us -> none  [local(): lax.psum_scatter(flat, ('row', 'col'), scatter_dimension=0, tiled=True)]
    ppermute x16 -> x0, starting transfers between devices: 76.2 us -> none  [the longest x8 53.1 us: padded_2(): lax.ppermute(head, axis, [((i + 1) % count, i) for i in range(count)])]
    pallas_call x0 -> x1, Pallas kernels: none -> 58.7 us  [local(): pl.pallas_call(kernel, out_shape=(jax.ShapeDtypeStruct((SIDE, SIDE, FEATS...]
    all_to_all x4 -> x0, starting transfers between devices: 21.3 us -> none  [the longest x1 7.74 us: local(): lax.all_to_all(packed_cols.reshape(owners, capacity, feats), 'grp', split...]
    ppermute x16 -> x0, waiting for transfers between devices: 12.3 us -> none  [the longest x8 12.3 us: padded_2(): lax.ppermute(tail, axis, [(i, (i + 1) % count) for i in range(count)])]
    dot_general x8 -> x0, matrix products: 7.98 us -> none  [the longest x1 1.98 us: local(): pre = jnp.dot(owner_cols, weight_in, preferred_element_type=jnp.float32)]
    all_to_all x4 -> x0, waiting for transfers between devices: 7.13 us -> none  [the longest x1 4.1 us: local(): lax.all_to_all(packed_cols.reshape(owners, capacity, feats), 'grp', split...]
    convert_element_type x10 -> x0, other arithmetic: 2.48 us -> none  [the longest x4 1.42 us: local(): field.astype(jnp.bfloat16)]
  transfers between devices with their start and end apart: 21 -> 0, of which waited for: 8 -> 0; matrix products, arithmetic and copies ran while one was open for 7% -> 0% of each run, Pallas kernels for 0% -> 0%
where the time goes in v1:
time: 62.7 us; the launch traced here: 62.5 us
  Pallas kernels  58.7 us (94%)
  local copies, waits for them, and re-layouts  3.08 us (5%)
  between operations  0.65 us (1%)
    pallas_call x1, Pallas kernels, local(): pl.pallas_call(kernel, out_shape=(jax.ShapeDtypeStruct((SIDE, SIDE, FEATS...  58.7 us
    unnamed x7, local copies, waits for them, and re-layouts  3.08 us

profile of v1, /device:TPU:1, one launch (start us, length us, event | category | flops | bytes accessed | tf_op | source)
XLA Modules:
  0.0 62.5 jit_solution(8202758634797006677)
XLA Ops:
  0.6 58.7 %window.1 = (f32[16,16,256]{2,1,0:T(8,128)}, bf16[16,16,256]{2,1,0:T(8,128)(2,1)}, f32[64,128]{1,0:T(8,128)}) custom-call(f32[16,16,256]{2,1,0:T(8,128)} %state_ref.1, f32[16,16]{1,0:T(8,128)} %rate_ref.1, bf16[16,16,256]{2,1,0:T(8,128)(2,1)} %cot_ref.1, s32[1,256]{1,0:T(1,128)} %bitcast.7, bf16[256,1024]{1,0:T(8,128)(2,1)} %bitcast.4, bf16[256,1024]{1,0:T(8,128)(2,1)} %bitcast.5), custom_call_target="tpu_custom_call" | custom-call | tf_op jit(solution)/shard_map/window/pallas_call | solution.py:359
  59.4 0.0 copy-start
  59.4 1.7 %copy.12 = f32[16,16,256]{2,1,0:T(8,128)} copy(f32[16,16,256]{2,1,0:T(8,128)} %get-tuple-element.12) | data formatting | bytes 524288
  61.1 0.0 copy-done
  61.1 0.0 copy-start.1
  61.1 0.7 %copy.13 = bf16[16,16,256]{2,1,0:T(8,128)(2,1)} copy(bf16[16,16,256]{2,1,0:T(8,128)(2,1)S(1)} %copy-done) | data formatting | bytes 262144
  61.7 0.1 copy-done.1
  61.8 0.6 copy.14
Async XLA Ops:
  59.4 1.7 %copy-start = (bf16[16,16,256]{2,1,0:T(8,128)(2,1)S(1)}, bf16[16,16,256]{2,1,0:T(8,128)(2,1)}, u32[]{:S(2)}) copy-start(bf16[16,16,256]{2,1,0:T(8,128)(2,1)} %get-tuple-element.13) | copy-start | bytes 393220
  61.1 0.8 %copy-start.1 = (f32[64,128]{1,0:T(8,128)S(1)}, f32[64,128]{1,0:T(8,128)}, u32[]{:S(2)}) copy-start(f32[64,128]{1,0:T(8,128)} %get-tuple-element.8) | copy-start | bytes 98308

commit v2 on v1

--- a/solution.py
+++ b/solution.py
@@ -30,6 +30,7 @@
 SIDES = [(0, 1), (0, -1), (1, 0), (-1, 0), (1, 1), (1, -1), (-1, 1), (-1, -1)]
 FAR_X = [4, 3, 5, 2, 6, 1, 7]
 FAR_Z = [2, 1, 3]
+PAIR = BF16
 
 
 def iota(shape, dim):
@@ -37,15 +38,19 @@
 
 
 def kernel(
-    state_ref,
-    rate_ref,
-    cot_ref,
-    dest_ref,
+    state_hbm,
+    rate_hbm,
+    cot_hbm,
+    dest_hbm,
     win_hbm,
     wout_hbm,
     new_ref,
     adj_ref,
     grad_ref,
+    state_ref,
+    rate_ref,
+    cot_ref,
+    dest_ref,
     win,
     wout,
     send,
@@ -71,7 +76,7 @@
     sum_z,
     out_z,
     x2,
-    w_sem,
+    in_sem,
     fwd_send,
     fwd_recv,
     back_send,
@@ -128,12 +133,22 @@
             src_ref=src, dst_ref=dst, send_sem=sent, recv_sem=came, device_id=there, device_id_type=MESH
         )
 
-    w_copies = [
-        pltpu.make_async_copy(win_hbm, win, w_sem.at[0]),
-        pltpu.make_async_copy(wout_hbm, wout, w_sem.at[1]),
-    ]
-    for copy in w_copies:
-        copy.start()
+    loads = [
+        pltpu.make_async_copy(src, dst, in_sem.at[n])
+        for n, (src, dst) in enumerate(
+            (
+                (dest_hbm, dest_ref),
+                (state_hbm, state_ref),
+                (cot_hbm, cot_ref),
+                (rate_hbm, rate_ref),
+                (win_hbm, win),
+                (wout_hbm, wout),
+            )
+        )
+    ]
+    for copy in loads:
+        copy.start()
+    loads[0].wait()
 
     dest = dest_ref[...]
     dy = ((dest >> 1) - y) & (NY - 1)
@@ -150,11 +165,13 @@
     placing = jnp.where(
         iota((SLOTS * CAP, COLUMNS), 0) == places.astype(I32), 1.0, 0.0
     ).astype(BF16)
+    loads[1].wait()
     cells = state_ref[...].astype(BF16)
     packed = jnp.dot(placing, cells.reshape(COLUMNS, FEATS), preferred_element_type=F32)
     packed = packed.astype(BF16).reshape(SLOTS, CAP, FEATS)
     send[:, :, 0:FEATS] = packed
     recv[0, :, 0:FEATS] = packed[0]
+    loads[2].wait()
     packed = 0.5 * jnp.dot(
         placing, cot_ref[...].reshape(COLUMNS, FEATS), preferred_element_type=F32
     )
@@ -162,6 +179,16 @@
     send[:, :, FEATS:] = packed
     recv[0, :, FEATS:] = packed[0]
 
+    pl.semaphore_wait(barrier, len(greeted))
+
+    fwd = {
+        t: remote(send.at[t], recv.at[t], fwd_send.at[t], fwd_recv.at[t], at_expert(*OFFSETS[t]))
+        for t in SENDING
+    }
+    for t in SENDING[:3]:
+        fwd[t].start()
+
+    loads[3].wait()
     edge[:, :, :, 0:FEATS] = cells.reshape(SIDE, 2, 8, FEATS)
     diagonal = iota((SIDE, SIDE), 0) == iota((SIDE, SIDE), 1)
     for i in range(SIDE):
@@ -170,15 +197,6 @@
         line = jnp.broadcast_to(line, (SIDE, 128))
         rates[4 + i, 8 : 8 + SIDE, :] = line
         edge[i, :, :, FEATS:] = line.astype(BF16).reshape(2, 8, 128)
-
-    pl.semaphore_wait(barrier, len(greeted))
-
-    fwd = {
-        t: remote(send.at[t], recv.at[t], fwd_send.at[t], fwd_recv.at[t], at_expert(*OFFSETS[t]))
-        for t in SENDING
-    }
-    for t in SENDING:
-        fwd[t].start()
 
     span = {-1: (slice(0, 4), slice(20, 24)), 1: (slice(12, 16), slice(0, 4)), 0: (slice(0, 16), slice(4, 20))}
     tile = {-1: (slice(0, 1), slice(3, 4)), 1: (slice(1, 2), slice(0, 1)), 0: (slice(0, 2), slice(1, 3))}
@@ -194,8 +212,10 @@
     ]
     for copy in edges:
         copy.start()
-
-    for copy in w_copies:
+    for t in SENDING[3:]:
+        fwd[t].start()
+
+    for copy in loads[4:]:
         copy.wait()
 
     homeward = {
@@ -206,6 +226,9 @@
         for t in range(4 * g, 4 * g + 4):
             if t:
                 fwd[t].wait_recv()
+        if g == 3:
+            for t in SENDING[:11]:
+                homeward[t].start()
         lines = slice(128 * g, 128 * g + 128)
         came = recv[4 * g : 4 * g + 4].reshape(128, 2 * FEATS)
         columns, dtend = came[:, 0:FEATS], came[:, FEATS:]
@@ -226,28 +249,54 @@
         if g == 0:
             home[0, :, 0:FEATS] = tend[0]
             home[0, :, FEATS:] = adjoint[0]
-        for t in range(4 * g, 4 * g + 4):
-            if t:
+        if g == 3:
+            for t in SENDING[11:]:
                 homeward[t].start()
 
+        if g == 1:
+            for copy in edges:
+                copy.wait_recv()
+            for top in (0, 20):
+                cells = halo[top : top + 4].astype(F32).reshape(4, 32, WIDE)
+                field_a[top : top + 4] = cells[:, :, 0:FEATS]
+                rates[top : top + 4] = cells[:, :, FEATS:]
+            for t in (0, 3):
+                cells = halo[4:20, t].astype(F32)
+                field_a[4:20, 8 * t : 8 * t + 8] = cells[:, :, 0:FEATS]
+                rates[4:20, 8 * t : 8 * t + 8] = cells[:, :, FEATS:]
+            field_a[4:20, 8:24] = state_ref[...]
+            old, new = field_a, field_b
+            for step in range(1, STEPS + 1):
+
+                def advance(n, carry, old=old, new=new, step=step):
+                    i = step + 2 * n
+                    here = old[pl.ds(i, 2)]
+                    beside = old[pl.ds(i - 1, 2)] + old[pl.ds(i + 1, 2)]
+                    beside = beside + pltpu.roll(here, 1, 1) + pltpu.roll(here, 31, 1)
+                    pace = rates[pl.ds(i, 2)]
+                    pace = jnp.concatenate([pace, pace], axis=2)
+                    new[pl.ds(i, 2)] = here + pace * (beside - 4.0 * here)
+                    return carry
+
+                lax.fori_loop(0, 12 - step, advance, 0)
+                old, new = new, old
+
+    parts = (slice(0, XF), slice(XF, HID))
     pairs = []
-    for n, (first, hidden) in enumerate(((FEATS, act_ref), (0, dpre_ref))):
-        left = recv[:, :, first : first + FEATS].reshape(SLOTS * CAP, FEATS)
-        out = slice(16 - 16 * n, 32 - 16 * n)
-        for h in range(0, HID, TN):
-            part = lax.dot_general(
-                left, hidden[:, h : h + TN], (((0,), (0,)), ((), ())), preferred_element_type=F32
-            )
-            grads[out, :, :, h : h + TN] = part.reshape(16, 2, 8, TN)
-        copy = remote(grads.at[out, 1 - col], pair.at[out], pair_send.at[n], pair_recv.at[n], partner)
+    for n, part in enumerate(parts):
+        for first, hidden, out in ((FEATS, act_ref, slice(16, 32)), (0, dpre_ref, slice(0, 16))):
+            left = recv[:, :, first : first + FEATS].reshape(SLOTS * CAP, FEATS)
+            for h in range(part.start, part.stop, TN):
+                width = min(TN, part.stop - h)
+                piece = lax.dot_general(
+                    left, hidden[:, h : h + width], (((0,), (0,)), ((), ())), preferred_element_type=F32
+                )
+                grads[out, :, :, h : h + width] = piece.reshape(16, 2, 8, width).astype(PAIR)
+        copy = remote(
+            grads.at[:, 1 - col, :, part], pair.at[:, :, part], pair_send.at[n], pair_recv.at[n], partner
+        )
         copy.start()
         pairs.append(copy)
-    for n, copy in enumerate(pairs):
-        copy.wait_recv()
-        out = slice(16 - 16 * n, 32 - 16 * n)
-        both = grads[out, col] + pair[out]
-        half[4 - 4 * n : 8 - 4 * n] = both.astype(BF16).reshape(4, NZ, 8, HID)
-
     first_x = [
         remote(
             half.at[(x + dx) % NX, :, :, 0:XF], x1.at[dx], x1_send.at[dx], x1_recv.at[dx], at_x(dx)
@@ -260,35 +309,12 @@
         )
         for dz in FAR_Z
     ]
-    for copy in first_x + first_z:
-        copy.start()
-
-    for copy in edges:
+    for part, copy, onward in zip(parts, pairs, (first_x, first_z)):
         copy.wait_recv()
-    for top in (0, 20):
-        cells = halo[top : top + 4].astype(F32).reshape(4, 32, WIDE)
-        field_a[top : top + 4] = cells[:, :, 0:FEATS]
-        rates[top : top + 4] = cells[:, :, FEATS:]
-    for t in (0, 3):
-        cells = halo[4:20, t].astype(F32)
-        field_a[4:20, 8 * t : 8 * t + 8] = cells[:, :, 0:FEATS]
-        rates[4:20, 8 * t : 8 * t + 8] = cells[:, :, FEATS:]
-    field_a[4:20, 8:24] = state_ref[...]
-    old, new = field_a, field_b
-    for step in range(1, STEPS + 1):
-
-        def advance(n, carry, old=old, new=new, step=step):
-            i = step + 2 * n
-            here = old[pl.ds(i, 2)]
-            beside = old[pl.ds(i - 1, 2)] + old[pl.ds(i + 1, 2)]
-            beside = beside + pltpu.roll(here, 1, 1) + pltpu.roll(here, 31, 1)
-            pace = rates[pl.ds(i, 2)]
-            pace = jnp.concatenate([pace, pace], axis=2)
-            new[pl.ds(i, 2)] = here + pace * (beside - 4.0 * here)
-            return carry
-
-        lax.fori_loop(0, 12 - step, advance, 0)
-        old, new = new, old
+        both = grads[:, col, :, part].astype(F32) + pair[:, :, part].astype(F32)
+        half[:, :, :, part] = both.astype(BF16).reshape(NX, NZ, 8, part.stop - part.start)
+        for there in onward:
+            there.start()
 
     for copy in first_x:
         copy.wait_recv()
@@ -352,20 +378,32 @@
         copy.wait_send()
 
 
+def put_out(*refs):
+    copies = [pltpu.make_async_copy(refs[n], refs[3 + n], refs[6].at[n]) for n in range(3)]
+    for copy in copies:
+        copy.start()
+    for copy in copies:
+        copy.wait()
+
+
 def local(state, rate, cotangent, dest, w_in, w_out):
     vmem = pl.BlockSpec(memory_space=pltpu.VMEM)
     hbm = pl.BlockSpec(memory_space=pl.ANY)
     sems = pltpu.SemaphoreType.DMA
-    new_state, adjoint, grads = pl.pallas_call(
+    results = pl.pallas_call(
         kernel,
         out_shape=(
-            jax.ShapeDtypeStruct((SIDE, SIDE, FEATS), F32),
-            jax.ShapeDtypeStruct((SIDE, SIDE, FEATS), BF16),
-            jax.ShapeDtypeStruct((HID // 128 * 8, 128), F32),
+            pltpu.VMEM((SIDE, SIDE, FEATS), F32),
+            pltpu.VMEM((SIDE, SIDE, FEATS), BF16),
+            pltpu.VMEM((HID // 128 * 8, 128), F32),
         ),
-        in_specs=[vmem, vmem, vmem, vmem, hbm, hbm],
+        in_specs=[hbm] * 6,
         out_specs=(vmem, vmem, vmem),
         scratch_shapes=[
+            pltpu.VMEM((SIDE, SIDE, FEATS), F32),
+            pltpu.VMEM((SIDE, SIDE), F32),
+            pltpu.VMEM((SIDE, SIDE, FEATS), BF16),
+            pltpu.VMEM((1, COLUMNS), I32),
             pltpu.VMEM((FEATS, HID), BF16),
             pltpu.VMEM((FEATS, HID), BF16),
             pltpu.VMEM((SLOTS, CAP, 2 * FEATS), BF16),
@@ -380,8 +418,8 @@
             pltpu.VMEM((24, 32, FEATS), F32),
             pltpu.VMEM((24, 32, FEATS), F32),
             pltpu.VMEM((24, 32, 128), F32),
-            pltpu.VMEM((32, 2, 8, HID), F32),
-            pltpu.VMEM((32, 8, HID), F32),
+            pltpu.VMEM((32, 2, 8, HID), PAIR),
+            pltpu.VMEM((32, 8, HID), PAIR),
             pltpu.VMEM((NX, NZ, 8, HID), BF16),
             pltpu.VMEM((NX, NZ, 8, XF), BF16),
             pltpu.VMEM((NZ, NX, 8, HID - XF), BF16),
@@ -391,7 +429,7 @@
             pltpu.VMEM((NX, 8, HID - XF), F32),
             pltpu.VMEM((NX, 8, HID - XF), BF16),
             pltpu.VMEM((NX, 8, HID - XF), BF16),
-            sems((2,)),
+            sems((6,)),
             sems((SLOTS,)),
             sems((SLOTS,)),
             sems((SLOTS,)),
@@ -412,6 +450,18 @@
         compiler_params=pltpu.CompilerParams(collective_id=0, has_side_effects=True),
         name="window",
     )(state, rate, cotangent, dest.reshape(1, COLUMNS), w_in[0], w_out[0])
+    new_state, adjoint, grads = pl.pallas_call(
+        put_out,
+        out_shape=(
+            jax.ShapeDtypeStruct((SIDE, SIDE, FEATS), F32),
+            jax.ShapeDtypeStruct((SIDE, SIDE, FEATS), BF16),
+            jax.ShapeDtypeStruct((HID // 128 * 8, 128), F32),
+        ),
+        in_specs=[vmem] * 3,
+        out_specs=(hbm,) * 3,
+        scratch_shapes=[sems((3,))],
+        name="put_out",
+    )(*(pltpu.with_memory_space_constraint(r, pltpu.VMEM) for r in results))
     return new_state, adjoint, grads[None]
 
 

time: 62.7 us -> 58.1 us (0.927)
  local copies, waits for them, and re-layouts: 3.08 us -> 0 us
  Pallas kernels: 58.7 us -> 57.1 us
    unnamed x7 -> x0, local copies, waits for them, and re-layouts: 3.08 us -> none
    pallas_call x1 -> x2, Pallas kernels: 58.7 us -> 57.1 us  [the longest x1 56.4 us: local(): pl.pallas_call(kernel, out_shape=(pltpu.VMEM((SIDE, SIDE, FEATS), F32), p...]
where the time goes in v2:
time: 58.1 us; the launch traced here: 57.8 us
  Pallas kernels  57.1 us (98%)
  between operations  0.64 us (1%)
    pallas_call x1, Pallas kernels, local(): pl.pallas_call(kernel, out_shape=(pltpu.VMEM((SIDE, SIDE, FEATS), F32), p...  56.4 us

profile of v2, /device:TPU:1, one launch (start us, length us, event | category | flops | bytes accessed | tf_op | source)
XLA Modules:
  0.0 57.8 jit_solution(16670992483284565979)
XLA Ops:
  0.6 56.4 %window.1 = (f32[16,16,256]{2,1,0:T(8,128)S(1)}, bf16[16,16,256]{2,1,0:T(8,128)(2,1)S(1)}, f32[64,128]{1,0:T(8,128)S(1)}) custom-call(f32[16,16,256]{2,1,0:T(8,128)} %state_hbm.1, f32[16,16]{1,0:T(8,128)} %rate_hbm.1, bf16[16,16,256]{2,1,0:T(8,128)(2,1)} %cot_hbm.1, s32[1,256]{1,0:T(1,128)} %bitcast.6, bf16[256,1024]{1,0:T(8,128)(2,1)} %bitcast.4, ...), custom_call_target="tpu_custom_call" | custom-call | tf_op jit(solution)/shard_map/window/pallas_call | solution.py:393
  57.0 0.8 %put_out.1 = (f32[16,16,256]{2,1,0:T(8,128)}, bf16[16,16,256]{2,1,0:T(8,128)(2,1)}, f32[64,128]{1,0:T(8,128)}) custom-call(f32[16,16,256]{2,1,0:T(8,128)S(1)} %get-tuple-element.9.refs_0_, bf16[16,16,256]{2,1,0:T(8,128)(2,1)S(1)} %get-tuple-element.10.refs_1_, f32[64,128]{1,0:T(8,128)S(1)} %get-tuple-element.11.refs_2_), custom_call_target="tpu_custom_call" | custom-call | tf_op jit(solution)/shard_map/put_out/pallas_call | solution.py:453

commit v3 on v2

--- a/solution.py
+++ b/solution.py
@@ -117,22 +117,6 @@
 
     partner = {"row": row, "grp": grp, "col": 1 - col}
 
-    barrier = pltpu.get_barrier_semaphore()
-    greeted = (
-        [at_expert(*OFFSETS[t]) for t in SENDING]
-        + [at_side(*o) for o in SIDES]
-        + [at_x(dx) for dx in FAR_X]
-        + [at_z(dz) for dz in FAR_Z]
-        + [partner]
-    )
-    for there in greeted:
-        pl.semaphore_signal(barrier, inc=1, device_id=there, device_id_type=MESH)
-
-    def remote(src, dst, sent, came, there):
-        return pltpu.make_async_remote_copy(
-            src_ref=src, dst_ref=dst, send_sem=sent, recv_sem=came, device_id=there, device_id_type=MESH
-        )
-
     loads = [
         pltpu.make_async_copy(src, dst, in_sem.at[n])
         for n, (src, dst) in enumerate(
@@ -148,6 +132,23 @@
     ]
     for copy in loads:
         copy.start()
+
+    barrier = pltpu.get_barrier_semaphore()
+    greeted = (
+        [at_expert(*OFFSETS[t]) for t in SENDING]
+        + [at_side(*o) for o in SIDES]
+        + [at_x(dx) for dx in FAR_X]
+        + [at_z(dz) for dz in FAR_Z]
+        + [partner]
+    )
+    for there in greeted:
+        pl.semaphore_signal(barrier, inc=1, device_id=there, device_id_type=MESH)
+
+    def remote(src, dst, sent, came, there):
+        return pltpu.make_async_remote_copy(
+            src_ref=src, dst_ref=dst, send_sem=sent, recv_sem=came, device_id=there, device_id_type=MESH
+        )
+
     loads[0].wait()
 
     dest = dest_ref[...]
@@ -222,6 +223,19 @@
         t: remote(back.at[t], home.at[t], back_send.at[t], back_recv.at[t], at_source(*OFFSETS[t]))
         for t in SENDING
     }
+    def answer(g):
+        lines = slice(128 * g, 128 * g + 128)
+        across = (((1,), (1,)), ((), ()))
+        tend = lax.dot_general(act_ref[lines, :], wout[...], across, preferred_element_type=F32)
+        adjoint = lax.dot_general(dpre_ref[lines, :], win[...], across, preferred_element_type=F32)
+        tend = tend.astype(BF16).reshape(4, CAP, FEATS)
+        adjoint = adjoint.astype(BF16).reshape(4, CAP, FEATS)
+        back[4 * g : 4 * g + 4, :, 0:FEATS] = tend
+        back[4 * g : 4 * g + 4, :, FEATS:] = adjoint
+        if g == 0:
+            home[0, :, 0:FEATS] = tend[0]
+            home[0, :, FEATS:] = adjoint[0]
+
     for g in range(4):
         for t in range(4 * g, 4 * g + 4):
             if t:
@@ -239,20 +253,8 @@
             act_ref[lines, h : h + TN] = (pre * sigma).astype(BF16)
             slope = sigma * (1.0 + pre * (1.0 - sigma))
             dpre_ref[lines, h : h + TN] = (dact * slope).astype(BF16)
-        across = (((1,), (1,)), ((), ()))
-        tend = lax.dot_general(act_ref[lines, :], wout[...], across, preferred_element_type=F32)
-        adjoint = lax.dot_general(dpre_ref[lines, :], win[...], across, preferred_element_type=F32)
-        tend = tend.astype(BF16).reshape(4, CAP, FEATS)
-        adjoint = adjoint.astype(BF16).reshape(4, CAP, FEATS)
-        back[4 * g : 4 * g + 4, :, 0:FEATS] = tend
-        back[4 * g : 4 * g + 4, :, FEATS:] = adjoint
-        if g == 0:
-            home[0, :, 0:FEATS] = tend[0]
-            home[0, :, FEATS:] = adjoint[0]
-        if g == 3:
-            for t in SENDING[11:]:
-                homeward[t].start()
-
+        if g < 3:
+            answer(g)
         if g == 1:
             for copy in edges:
                 copy.wait_recv()
@@ -297,6 +299,9 @@
         )
         copy.start()
         pairs.append(copy)
+    answer(3)
+    for t in SENDING[11:]:
+        homeward[t].start()
     first_x = [
         remote(
             half.at[(x + dx) % NX, :, :, 0:XF], x1.at[dx], x1_send.at[dx], x1_recv.at[dx], at_x(dx)

time: 58.1 us -> 57.9 us (level)
  no operation moved by 1% of the time
where the time goes in v3:
time: 57.9 us; the launch traced here: 57.8 us
  Pallas kernels  57.1 us (99%)
  between operations  0.64 us (1%)
    pallas_call x1, Pallas kernels, local(): pl.pallas_call(kernel, out_shape=(pltpu.VMEM((SIDE, SIDE, FEATS), F32), p...  56.4 us

profile of v3, /device:TPU:1, one launch (start us, length us, event | category | flops | bytes accessed | tf_op | source)
XLA Modules:
  0.0 57.8 jit_solution(17376647562949259452)
XLA Ops:
  0.6 56.4 %window.1 = (f32[16,16,256]{2,1,0:T(8,128)S(1)}, bf16[16,16,256]{2,1,0:T(8,128)(2,1)S(1)}, f32[64,128]{1,0:T(8,128)S(1)}) custom-call(f32[16,16,256]{2,1,0:T(8,128)} %state_hbm.1, f32[16,16]{1,0:T(8,128)} %rate_hbm.1, bf16[16,16,256]{2,1,0:T(8,128)(2,1)} %cot_hbm.1, s32[1,256]{1,0:T(1,128)} %bitcast.6, bf16[256,1024]{1,0:T(8,128)(2,1)} %bitcast.4, ...), custom_call_target="tpu_custom_call" | custom-call | tf_op jit(solution)/shard_map/window/pallas_call | solution.py:398
  57.0 0.8 %put_out.1 = (f32[16,16,256]{2,1,0:T(8,128)}, bf16[16,16,256]{2,1,0:T(8,128)(2,1)}, f32[64,128]{1,0:T(8,128)}) custom-call(f32[16,16,256]{2,1,0:T(8,128)S(1)} %get-tuple-element.9.refs_0_, bf16[16,16,256]{2,1,0:T(8,128)(2,1)S(1)} %get-tuple-element.10.refs_1_, f32[64,128]{1,0:T(8,128)S(1)} %get-tuple-element.11.refs_2_), custom_call_target="tpu_custom_call" | custom-call | tf_op jit(solution)/shard_map/put_out/pallas_call | solution.py:458

commit v4 on v3

--- a/solution.py
+++ b/solution.py
@@ -18,7 +18,6 @@
 NY, NL = 8, 2
 SLOTS = NY * NL
 COLUMNS = SIDE * SIDE
-WIDE = FEATS + 128
 XF = 640
 TN = 256
 
@@ -62,6 +61,8 @@
     dpre_ref,
     edge,
     halo,
+    pace_out,
+    pace_in,
     field_a,
     field_b,
     rates,
@@ -83,6 +84,8 @@
     back_recv,
     edge_send,
     edge_recv,
+    pace_send,
+    pace_recv,
     pair_send,
     pair_recv,
     x1_send,
@@ -190,14 +193,9 @@
         fwd[t].start()
 
     loads[3].wait()
-    edge[:, :, :, 0:FEATS] = cells.reshape(SIDE, 2, 8, FEATS)
-    diagonal = iota((SIDE, SIDE), 0) == iota((SIDE, SIDE), 1)
-    for i in range(SIDE):
-        line = jnp.broadcast_to(rate_ref[i : i + 1, :], (SIDE, SIDE))
-        line = jnp.sum(jnp.where(diagonal, line, 0.0), axis=1, keepdims=True)
-        line = jnp.broadcast_to(line, (SIDE, 128))
-        rates[4 + i, 8 : 8 + SIDE, :] = line
-        edge[i, :, :, FEATS:] = line.astype(BF16).reshape(2, 8, 128)
+    edge[...] = cells.reshape(SIDE, 2, 8, FEATS)
+    pace_out[...] = jnp.zeros_like(pace_out)
+    pace_out[:, 0:SIDE] = rate_ref[...]
 
     span = {-1: (slice(0, 4), slice(20, 24)), 1: (slice(12, 16), slice(0, 4)), 0: (slice(0, 16), slice(4, 20))}
     tile = {-1: (slice(0, 1), slice(3, 4)), 1: (slice(1, 2), slice(0, 1)), 0: (slice(0, 2), slice(1, 3))}
@@ -211,10 +209,14 @@
         )
         for n, (di, dj) in enumerate(SIDES)
     ]
-    for copy in edges:
-        copy.start()
+    paces = [
+        remote(pace_out, pace_in.at[n], pace_send.at[n], pace_recv.at[n], at_side(*o))
+        for n, o in enumerate(SIDES)
+    ]
     for t in SENDING[3:]:
         fwd[t].start()
+    for copy in edges + paces:
+        copy.start()
 
     for copy in loads[4:]:
         copy.wait()
@@ -223,6 +225,12 @@
         t: remote(back.at[t], home.at[t], back_send.at[t], back_recv.at[t], at_source(*OFFSETS[t]))
         for t in SENDING
     }
+    def spread(line, first, i, j, width):
+        own = iota((width, 128), 1) == iota((width, 128), 0) + first
+        line = jnp.where(own, jnp.broadcast_to(line, (width, 128)), 0.0)
+        line = jnp.sum(line, axis=1, keepdims=True)
+        rates[i, j : j + width, :] = jnp.broadcast_to(line, (width, 128))
+
     def answer(g):
         lines = slice(128 * g, 128 * g + 128)
         across = (((1,), (1,)), ((), ()))
@@ -255,33 +263,6 @@
             dpre_ref[lines, h : h + TN] = (dact * slope).astype(BF16)
         if g < 3:
             answer(g)
-        if g == 1:
-            for copy in edges:
-                copy.wait_recv()
-            for top in (0, 20):
-                cells = halo[top : top + 4].astype(F32).reshape(4, 32, WIDE)
-                field_a[top : top + 4] = cells[:, :, 0:FEATS]
-                rates[top : top + 4] = cells[:, :, FEATS:]
-            for t in (0, 3):
-                cells = halo[4:20, t].astype(F32)
-                field_a[4:20, 8 * t : 8 * t + 8] = cells[:, :, 0:FEATS]
-                rates[4:20, 8 * t : 8 * t + 8] = cells[:, :, FEATS:]
-            field_a[4:20, 8:24] = state_ref[...]
-            old, new = field_a, field_b
-            for step in range(1, STEPS + 1):
-
-                def advance(n, carry, old=old, new=new, step=step):
-                    i = step + 2 * n
-                    here = old[pl.ds(i, 2)]
-                    beside = old[pl.ds(i - 1, 2)] + old[pl.ds(i + 1, 2)]
-                    beside = beside + pltpu.roll(here, 1, 1) + pltpu.roll(here, 31, 1)
-                    pace = rates[pl.ds(i, 2)]
-                    pace = jnp.concatenate([pace, pace], axis=2)
-                    new[pl.ds(i, 2)] = here + pace * (beside - 4.0 * here)
-                    return carry
-
-                lax.fori_loop(0, 12 - step, advance, 0)
-                old, new = new, old
 
     parts = (slice(0, XF), slice(XF, HID))
     pairs = []
@@ -321,6 +302,41 @@
         for there in onward:
             there.start()
 
+    for i in range(SIDE):
+        spread(pace_out[i : i + 1, :], 0, 4 + i, 8, SIDE)
+    for copy in edges + paces:
+        copy.wait_recv()
+    for n, (di, dj) in enumerate(SIDES):
+        (source, target), (left, right) = span[di], tile[dj]
+        for i in range(target.stop - target.start):
+            spread(
+                pace_in[n, source.start + i : source.start + i + 1, :],
+                8 * left.start,
+                target.start + i,
+                8 * right.start,
+                8 * (right.stop - right.start),
+            )
+    for top in (0, 20):
+        field_a[top : top + 4] = halo[top : top + 4].astype(F32).reshape(4, 32, FEATS)
+    for t in (0, 3):
+        field_a[4:20, 8 * t : 8 * t + 8] = halo[4:20, t].astype(F32)
+    field_a[4:20, 8:24] = state_ref[...]
+    old, new = field_a, field_b
+    for step in range(1, STEPS + 1):
+
+        def advance(n, carry, old=old, new=new, step=step):
+            i = step + 2 * n
+            here = old[pl.ds(i, 2)]
+            beside = old[pl.ds(i - 1, 2)] + old[pl.ds(i + 1, 2)]
+            beside = beside + pltpu.roll(here, 1, 1) + pltpu.roll(here, 31, 1)
+            pace = rates[pl.ds(i, 2)]
+            pace = jnp.concatenate([pace, pace], axis=2)
+            new[pl.ds(i, 2)] = here + pace * (beside - 4.0 * here)
+            return carry
+
+        lax.fori_loop(0, 12 - step, advance, 0)
+        old, new = new, old
+
     for copy in first_x:
         copy.wait_recv()
     total = half[x, :, :, 0:XF].astype(F32)
@@ -379,7 +395,7 @@
     for t in SENDING:
         fwd[t].wait_send()
         homeward[t].wait_send()
-    for copy in edges + pairs + first_x + first_z + last_x + last_z:
+    for copy in edges + paces + pairs + first_x + first_z + last_x + last_z:
         copy.wait_send()
 
 
@@ -418,8 +434,10 @@
             pltpu.VMEM((1, COLUMNS), F32),
             pltpu.VMEM((SLOTS * CAP, HID), BF16),
             pltpu.VMEM((SLOTS * CAP, HID), BF16),
-            pltpu.VMEM((SIDE, 2, 8, WIDE), BF16),
-            pltpu.VMEM((24, 4, 8, WIDE), BF16),
+            pltpu.VMEM((SIDE, 2, 8, FEATS), BF16),
+            pltpu.VMEM((24, 4, 8, FEATS), BF16),
+            pltpu.VMEM((SIDE, 128), F32),
+            pltpu.VMEM((8, SIDE, 128), F32),
             pltpu.VMEM((24, 32, FEATS), F32),
             pltpu.VMEM((24, 32, FEATS), F32),
             pltpu.VMEM((24, 32, 128), F32),
@@ -439,6 +457,8 @@
             sems((SLOTS,)),
             sems((SLOTS,)),
             sems((SLOTS,)),
+            sems((8,)),
+            sems((8,)),
             sems((8,)),
             sems((8,)),
             sems((2,)),

time: 57.9 us -> 57 us (0.984)
  Pallas kernels: 57.1 us -> 56.2 us
    pallas_call x1, Pallas kernels: 56.4 us -> 55.5 us  [local(): pl.pallas_call(kernel, out_shape=(pltpu.VMEM((SIDE, SIDE, FEATS), F32), p...]
where the time goes in v4:
time: 57 us; the launch traced here: 56.9 us
  Pallas kernels  56.2 us (99%)
  between operations  0.64 us (1%)
    pallas_call x1, Pallas kernels, local(): pl.pallas_call(kernel, out_shape=(pltpu.VMEM((SIDE, SIDE, FEATS), F32), p...  55.5 us

profile of v4, /device:TPU:1, one launch (start us, length us, event | category | flops | bytes accessed | tf_op | source)
XLA Modules:
  0.0 56.9 jit_solution(11160827223378521306)
XLA Ops:
  0.6 55.5 %window.1 = (f32[16,16,256]{2,1,0:T(8,128)S(1)}, bf16[16,16,256]{2,1,0:T(8,128)(2,1)S(1)}, f32[64,128]{1,0:T(8,128)S(1)}) custom-call(f32[16,16,256]{2,1,0:T(8,128)} %state_hbm.1, f32[16,16]{1,0:T(8,128)} %rate_hbm.1, bf16[16,16,256]{2,1,0:T(8,128)(2,1)} %cot_hbm.1, s32[1,256]{1,0:T(1,128)} %bitcast.6, bf16[256,1024]{1,0:T(8,128)(2,1)} %bitcast.4, ...), custom_call_target="tpu_custom_call" | custom-call | tf_op jit(solution)/shard_map/window/pallas_call | solution.py:414
  56.1 0.8 %put_out.1 = (f32[16,16,256]{2,1,0:T(8,128)}, bf16[16,16,256]{2,1,0:T(8,128)(2,1)}, f32[64,128]{1,0:T(8,128)}) custom-call(f32[16,16,256]{2,1,0:T(8,128)S(1)} %get-tuple-element.9.refs_0_, bf16[16,16,256]{2,1,0:T(8,128)(2,1)S(1)} %get-tuple-element.10.refs_1_, f32[64,128]{1,0:T(8,128)S(1)} %get-tuple-element.11.refs_2_), custom_call_target="tpu_custom_call" | custom-call | tf_op jit(solution)/shard_map/put_out/pallas_call | solution.py:478

commit v5 on v4

--- a/solution.py
+++ b/solution.py
@@ -189,7 +189,7 @@
         t: remote(send.at[t], recv.at[t], fwd_send.at[t], fwd_recv.at[t], at_expert(*OFFSETS[t]))
         for t in SENDING
     }
-    for t in SENDING[:3]:
+    for t in SENDING:
         fwd[t].start()
 
     loads[3].wait()
@@ -213,8 +213,6 @@
         remote(pace_out, pace_in.at[n], pace_send.at[n], pace_recv.at[n], at_side(*o))
         for n, o in enumerate(SIDES)
     ]
-    for t in SENDING[3:]:
-        fwd[t].start()
     for copy in edges + paces:
         copy.start()
 

time: 57 us -> 57.9 us (1.016); the launches traced: 56.9 us -> 56.9 us
  no operation moved by 1% of the time
where the time goes in v5:
time: 57.9 us; the launch traced here: 56.9 us
  Pallas kernels  56.2 us (97%)
  between operations  0.64 us (1%)
    pallas_call x1, Pallas kernels, local(): pl.pallas_call(kernel, out_shape=(pltpu.VMEM((SIDE, SIDE, FEATS), F32), p...  55.5 us

profile of v5, /device:TPU:1, one launch (start us, length us, event | category | flops | bytes accessed | tf_op | source)
XLA Modules:
  0.0 56.9 jit_solution(685281204905069343)
XLA Ops:
  0.6 55.5 %window.1 = (f32[16,16,256]{2,1,0:T(8,128)S(1)}, bf16[16,16,256]{2,1,0:T(8,128)(2,1)S(1)}, f32[64,128]{1,0:T(8,128)S(1)}) custom-call(f32[16,16,256]{2,1,0:T(8,128)} %state_hbm.1, f32[16,16]{1,0:T(8,128)} %rate_hbm.1, bf16[16,16,256]{2,1,0:T(8,128)(2,1)} %cot_hbm.1, s32[1,256]{1,0:T(1,128)} %bitcast.6, bf16[256,1024]{1,0:T(8,128)(2,1)} %bitcast.4, ...), custom_call_target="tpu_custom_call" | custom-call | tf_op jit(solution)/shard_map/window/pallas_call | solution.py:412
  56.1 0.8 %put_out.1 = (f32[16,16,256]{2,1,0:T(8,128)}, bf16[16,16,256]{2,1,0:T(8,128)(2,1)}, f32[64,128]{1,0:T(8,128)}) custom-call(f32[16,16,256]{2,1,0:T(8,128)S(1)} %get-tuple-element.9.refs_0_, bf16[16,16,256]{2,1,0:T(8,128)(2,1)S(1)} %get-tuple-element.10.refs_1_, f32[64,128]{1,0:T(8,128)S(1)} %get-tuple-element.11.refs_2_), custom_call_target="tpu_custom_call" | custom-call | tf_op jit(solution)/shard_map/put_out/pallas_call | solution.py:476

commit v6 on v4

--- a/solution.py
+++ b/solution.py
@@ -248,8 +248,8 @@
         for t in range(4 * g, 4 * g + 4):
             if t:
                 fwd[t].wait_recv()
-        if g == 3:
-            for t in SENDING[:11]:
+        if g >= 2:
+            for t in SENDING[3 * g - 6 : 8 * g - 13]:
                 homeward[t].start()
         lines = slice(128 * g, 128 * g + 128)
         came = recv[4 * g : 4 * g + 4].reshape(128, 2 * FEATS)

time: 57 us -> 58.3 us (1.023)
  Pallas kernels: 56.2 us -> 57.4 us
    pallas_call x1, Pallas kernels: 55.5 us -> 56.6 us  [local(): pl.pallas_call(kernel, out_shape=(pltpu.VMEM((SIDE, SIDE, FEATS), F32), p...]
where the time goes in v6:
time: 58.3 us; the launch traced here: 58 us
  Pallas kernels  57.4 us (98%)
  between operations  0.64 us (1%)
    pallas_call x1, Pallas kernels, local(): pl.pallas_call(kernel, out_shape=(pltpu.VMEM((SIDE, SIDE, FEATS), F32), p...  56.6 us

profile of v6, /device:TPU:1, one launch (start us, length us, event | category | flops | bytes accessed | tf_op | source)
XLA Modules:
  0.0 58.0 jit_solution(13965867797230625820)
XLA Ops:
  0.6 56.6 %window.1 = (f32[16,16,256]{2,1,0:T(8,128)S(1)}, bf16[16,16,256]{2,1,0:T(8,128)(2,1)S(1)}, f32[64,128]{1,0:T(8,128)S(1)}) custom-call(f32[16,16,256]{2,1,0:T(8,128)} %state_hbm.1, f32[16,16]{1,0:T(8,128)} %rate_hbm.1, bf16[16,16,256]{2,1,0:T(8,128)(2,1)} %cot_hbm.1, s32[1,256]{1,0:T(1,128)} %bitcast.6, bf16[256,1024]{1,0:T(8,128)(2,1)} %bitcast.4, ...), custom_call_target="tpu_custom_call" | custom-call | tf_op jit(solution)/shard_map/window/pallas_call | solution.py:414
  57.3 0.8 %put_out.1 = (f32[16,16,256]{2,1,0:T(8,128)}, bf16[16,16,256]{2,1,0:T(8,128)(2,1)}, f32[64,128]{1,0:T(8,128)}) custom-call(f32[16,16,256]{2,1,0:T(8,128)S(1)} %get-tuple-element.9.refs_0_, bf16[16,16,256]{2,1,0:T(8,128)(2,1)S(1)} %get-tuple-element.10.refs_1_, f32[64,128]{1,0:T(8,128)S(1)} %get-tuple-element.11.refs_2_), custom_call_target="tpu_custom_call" | custom-call | tf_op jit(solution)/shard_map/put_out/pallas_call | solution.py:478
